TPU v7x, 32 devices: a whole 2x2x4 slice. The times are simulated.
32 devices in a mesh: grid: 4 (over z), elec: 8 (over y, x, core).
Axes of the slice: x: 2, y: 2, z: 4, core: 2. Of those that a mesh axis runs over, the one named last changes fastest.
Arguments:
- electric: bfloat16 [2, 8192, 8192], P(None, 'elec', 'grid'), may hold values from -6 to 6
- trial: bfloat16 [8192, 2, 128], P('grid'), may hold values from -0.0625 to 0.0625
- counts: int32 [8], replicated, may hold values from 1 to 1024, as said below
Outputs:
- field: float32 [8192, 2, 128], P(('grid', 'elec'))
Inputs may be any that keep to these rules, and one draw needn't show every extreme that they name: `counts`: at least one group holds exactly 1024 live electrons.
All inputs are finite; a program needn't handle non-finite values.
Results may differ from a plain program's by a relative error of at most 0.0023.
Values sent between devices are 32-bit elements; how exact they have to be, the bound alone decides.
A program may use at most 64 MiB of HBM per device.

v0:
```python
import jax
import jax.numpy as jnp
from jax import lax
from jax.sharding import PartitionSpec as P


def margin_block(electric_slab, trial_flat, mode_count):
    slab_count = electric_slab.shape[1]
    flattened = electric_slab.reshape(2 * slab_count, electric_slab.shape[2])
    products = jnp.dot(flattened, trial_flat, preferred_element_type=jnp.float32)
    real_part = products[:slab_count, :mode_count] + products[slab_count:, mode_count:]
    imag_part = products[:slab_count, mode_count:] - products[slab_count:, :mode_count]
    return jnp.stack([real_part, imag_part])


def field_block(electric_slab, coef_real, coef_imag):
    slab_count = electric_slab.shape[1]
    flattened = electric_slab.reshape(2 * slab_count, electric_slab.shape[2])
    coef_matrix = jnp.concatenate(
        [jnp.concatenate([coef_real, coef_imag], 1), jnp.concatenate([-coef_imag, coef_real], 1)], 0
    )
    return lax.dot_general(
        flattened, coef_matrix, (((0,), (0,)), ((), ())), preferred_element_type=jnp.float32
    )


def body(electric, trial, counts):
    capacity = electric.shape[1]
    points = electric.shape[2]
    mode_count = trial.shape[2]
    trial_flat = trial.reshape(points, 2 * mode_count)
    group_index = lax.axis_index("elec")
    live_count = lax.dynamic_slice_in_dim(counts, group_index, 1, 0)[0]
    total_live = jnp.sum(counts.astype(jnp.float32))
    partial_margins = margin_block(electric, trial_flat, mode_count)
    margins = lax.psum(partial_margins, "grid")
    slot_ids = jnp.arange(capacity, dtype=jnp.int32)
    weights = jnp.where(slot_ids < live_count, 1.0, 0.0).astype(jnp.float32) * (
        1.0 / jnp.sqrt(total_live)
    )
    coefs = (margins * weights[None, :, None]).astype(jnp.bfloat16)
    coef_real = coefs[0]
    coef_imag = coefs[1]
    share = points // lax.axis_size("elec")
    mine = lax.psum_scatter(
        field_block(electric, coef_real, coef_imag), "elec", scatter_dimension=0, tiled=True
    )
    return mine.reshape(share, 2, mode_count)


def solution(mesh):
    placed = (P(None, "elec", "grid"), P("grid", None, None), P())
    return jax.shard_map(
        body, mesh=mesh, in_specs=placed, out_specs=P(("grid", "elec"), None, None), check_vma=False
    )
```

profile of v0, /device:TPU:0, one launch (start us, length us, event | category | flops | bytes accessed | tf_op | source)
XLA Modules:
  0.0 126.5 jit_solution(7639683581927419735)
XLA Ops:
  6.5 0.0 all-reduce.2.cloned.1.call-start
  6.5 6.1 %fusion = f32[2048,256]{1,0:T(8,128)S(1)} fusion(bf16[2048,2048]{1,0:T(8,128)(2,1)} %bitcast.22, bf16[256,8,2,128]{3,2,1,0:T(2,128)(2,1)} %bitcast.24), kind=kOutput, calls=%fused_computation.1 | convolution fusion | flops 2147483648 | bytes 11534336 | tf_op jit(solution)/shard_map/dot_general | solution.py:10
  12.6 0.1 fusion.11
  12.7 0.0 copy-start
  12.7 1.1 pad_maximum_fusion
  13.8 0.0 all-reduce.2.cloned.1.call-update
  13.9 0.0 reduce-scatter.2.cloned.1.call-start
  13.9 0.0 copy-done
  13.9 0.6 convert_reduce_fusion
  15.2 0.6 dynamic_slice.3
  15.8 0.6 select_multiply_fusion
  16.5 52.2 %all-reduce.2.cloned.1.call-done = f32[2,1024,128]{2,1,0:T(8,128)} async-done(((f32[2,1024,128]{2,1,0:T(8,128)}), f32[2,1024,128]{2,1,0:T(8,128)}) %all-reduce.2.cloned.1.call-update) | async-done | bytes 1048592 | tf_op jit(solution)/shard_map/psum | solution.py:36
  68.7 1.4 %multiply_convert_fusion = bf16[2,1024,128]{2,1,0:T(8,128)(2,1)S(1)} fusion(f32[2,1024,128]{2,1,0:T(8,128)} %all-reduce.2.cloned.1.call-done, f32[1024]{0:T(1024)S(1)} %select_multiply_fusion), kind=kLoop, calls=%fused_computation.12 | loop fusion | flops 524288 | bytes 1576960 | tf_op jit(solution)/shard_map/convert_element_type | solution.py:41
  70.2 7.1 %convolution_bitcast_fusion = f32[2048,256]{0,1:T(8,128)} fusion(bf16[2048,2048]{1,0:T(8,128)(2,1)} %bitcast.23, bf16[1024,128]{1,0:T(8,128)(2,1)S(1)} %get-tuple-element.8, bf16[1024,128]{1,0:T(8,128)(2,1)S(1)} %fusion.13, bf16[1024,128]{1,0:T(8,128)(2,1)S(1)} %get-tuple-element.7), kind=kOutput, calls=%fused_computation | convolution fusion | flops 2151677952 | bytes 11272192 | tf_op jit(solution)/shard_map/dot_general | solution.py:22
  77.3 0.0 reduce-scatter.2.cloned.1.call-update
  77.3 40.5 %reduce-scatter.2.cloned.1.call-done = f32[256,256]{0,1:T(8,128)} async-done(((f32[2048,256]{0,1:T(8,128)}), f32[256,256]{0,1:T(8,128)}) %reduce-scatter.2.cloned.1.call-update) | async-done | bytes 262160 | tf_op jit(solution)/shard_map/reduce_scatter | solution.py:45
  117.8 1.8 %copy.4 = f32[256,2,128]{2,1,0:T(2,128)} copy(f32[256,2,128]{0,2,1:T(8,128)} %bitcast.21) | data formatting | bytes 524288 | tf_op jit(solution)/shard_map/reshape | solution.py:48
  (2 shorter events, 0.1 us)
Async XLA Ops:
  6.5 62.1 %all-reduce.2.cloned.1.call-start = ((), (), s32[]{:S(2)}) async-start(), calls=%async_computation.1 | async-start | bytes 2097152 | tf_op jit(solution)/shard_map/psum | solution.py:36
  12.7 1.2 copy-start
  13.9 104.0 %reduce-scatter.2.cloned.1.call-start = ((), (), s32[]{:S(2)}) async-start(), calls=%async_computation.2 | async-start | bytes 2359296 | tf_op jit(solution)/shard_map/reduce_scatter | solution.py:45
Sparse Core Ops, SparseCore 0:
  14.0 54.6 all-reduce.1
  77.4 40.3 reduce-scatter.1
where the time goes:
time: 127 us; the launch traced here: 126 us
  waiting for transfers between devices  92.7 us (73%)
  between operations  14.2 us (11%)
  matrix products  13.2 us (10%)
  other arithmetic  3.91 us (3%)
  local copies, waits for them, and re-layouts  2.41 us (2%)
    psum x1, waiting for transfers between devices, body(): margins = lax.psum(partial_margins, 'grid')  52.2 us
    reduce_scatter x1, waiting for transfers between devices, body(): lax.psum_scatter(field_block(electric, coef_real, coef_imag), 'elec', sca...  40.5 us
    dot_general x1, matrix products, field_block(): lax.dot_general(flattened, coef_matrix, (((0,), (0,)), ((), ())), preferr...  7.11 us
    dot_general x1, matrix products, margin_block(): jnp.dot(flattened, trial_flat, preferred_element_type=jnp.float32)  6.08 us
  transfers between devices with their start and end apart: 2, of which 2 were waited for; matrix products, arithmetic and copies ran while one was open for 1% of the time, Pallas kernels for 0%

commit v1 on v0

--- a/solution.py
+++ b/solution.py
@@ -33,7 +33,7 @@
     live_count = lax.dynamic_slice_in_dim(counts, group_index, 1, 0)[0]
     total_live = jnp.sum(counts.astype(jnp.float32))
     partial_margins = margin_block(electric, trial_flat, mode_count)
-    margins = lax.psum(partial_margins, "grid")
+    margins = jnp.sum(lax.all_gather(partial_margins, "grid"), axis=0)
     slot_ids = jnp.arange(capacity, dtype=jnp.int32)
     weights = jnp.where(slot_ids < live_count, 1.0, 0.0).astype(jnp.float32) * (
         1.0 / jnp.sqrt(total_live)

time: 127 us -> 156 us (1.23)
  waiting for transfers between devices: 92.7 us -> 121 us
    all_gather x0 -> x1, waiting for transfers between devices: none -> 81 us  [body(): margins = jnp.sum(lax.all_gather(partial_margins, 'grid'), axis=0)]
    psum x1 -> x0, waiting for transfers between devices: 52.2 us -> none  [body(): margins = lax.psum(partial_margins, 'grid')]
    reduce_sum x0 -> x1, other arithmetic: none -> 2.56 us  [body(): margins = jnp.sum(lax.all_gather(partial_margins, 'grid'), axis=0)]
where the time goes in v1:
time: 156 us
  waiting for transfers between devices  121 us (78%)
  between operations  14.2 us (9%)
  matrix products  13.2 us (8%)
  other arithmetic  5.19 us (3%)
  local copies, waits for them, and re-layouts  2.41 us (2%)
    all_gather x1, waiting for transfers between devices, body(): margins = jnp.sum(lax.all_gather(partial_margins, 'grid'), axis=0)  81 us
    reduce_scatter x1, waiting for transfers between devices, body(): lax.psum_scatter(field_block(electric, coef_real, coef_imag), 'elec', sca...  39.8 us
    dot_general x1, matrix products, field_block(): lax.dot_general(flattened, coef_matrix, (((0,), (0,)), ((), ())), preferr...  7.1 us
    dot_general x1, matrix products, margin_block(): jnp.dot(flattened, trial_flat, preferred_element_type=jnp.float32)  6.08 us
  transfers between devices with their start and end apart: 2, of which 2 were waited for; matrix products, arithmetic and copies ran while one was open for 1% of the time, Pallas kernels for 0%

profile of v1, /device:TPU:0, one launch (start us, length us, event | category | flops | bytes accessed | tf_op | source)
XLA Modules:
  0.0 155.8 jit_solution(13078052573977622752)
XLA Ops:
  6.5 0.0 all-gather.3.cloned.1.call-start
  6.5 6.1 %fusion = f32[2048,256]{1,0:T(8,128)S(1)} fusion(bf16[2048,2048]{1,0:T(8,128)(2,1)} %bitcast.24, bf16[256,8,2,128]{3,2,1,0:T(2,128)(2,1)} %bitcast.26), kind=kOutput, calls=%fused_computation.1 | convolution fusion | flops 2147483648 | bytes 11534336 | tf_op jit(solution)/shard_map/dot_general | solution.py:10
  12.6 0.1 fusion.11
  12.7 0.0 copy-start
  12.7 1.0 pad_maximum_fusion
  13.8 0.0 all-gather.3.cloned.1.call-update
  13.8 0.0 reduce-scatter.2.cloned.1.call-start
  13.9 0.0 copy-done
  13.9 0.6 convert_reduce_fusion
  15.2 0.6 dynamic_slice.3
  15.8 0.6 select_multiply_fusion
  16.4 81.0 %all-gather.3.cloned.1.call-done = f32[8,1024,128]{2,1,0:T(8,128)} async-done(((f32[2,1024,128]{2,1,0:T(8,128)}), f32[8,1024,128]{2,1,0:T(8,128)}) %all-gather.3.cloned.1.call-update) | async-done | bytes 4194320 | tf_op jit(solution)/shard_map/all_gather | solution.py:36
  97.5 2.6 %reduce_sum.18 = f32[2,1024,128]{2,1,0:T(8,128)S(1)} reduce(f32[4,2,1024,128]{3,2,1,0:T(8,128)} %bitcast.22, f32[]{:T(128)} %constant.5.clone.1), dimensions={0}, to_apply=%region_0.0 | reduce | flops 786432 | bytes 5242884 | tf_op jit(solution)/shard_map/reduce_sum | solution.py:36
  100.0 0.2 multiply_convert_fusion
  100.3 7.1 %convolution_bitcast_fusion = f32[2048,256]{0,1:T(8,128)} fusion(bf16[2048,2048]{1,0:T(8,128)(2,1)} %bitcast.25, bf16[1024,128]{1,0:T(8,128)(2,1)S(1)} %get-tuple-element.8, bf16[1024,128]{1,0:T(8,128)(2,1)S(1)} %fusion.13, bf16[1024,128]{1,0:T(8,128)(2,1)S(1)} %get-tuple-element.7), kind=kOutput, calls=%fused_computation | convolution fusion | flops 2151677952 | bytes 11272192 | tf_op jit(solution)/shard_map/dot_general | solution.py:22
  107.4 0.0 reduce-scatter.2.cloned.1.call-update
  107.5 39.8 %reduce-scatter.2.cloned.1.call-done = f32[256,256]{0,1:T(8,128)} async-done(((f32[2048,256]{0,1:T(8,128)}), f32[256,256]{0,1:T(8,128)}) %reduce-scatter.2.cloned.1.call-update) | async-done | bytes 262160 | tf_op jit(solution)/shard_map/reduce_scatter | solution.py:45
  147.2 1.8 %copy.5 = f32[256,2,128]{2,1,0:T(2,128)} copy(f32[256,2,128]{0,2,1:T(8,128)} %bitcast.23) | data formatting | bytes 524288 | tf_op jit(solution)/shard_map/reshape | solution.py:48
  (2 shorter events, 0.1 us)
Async XLA Ops:
  6.5 90.9 %all-gather.3.cloned.1.call-start = ((), (), s32[]{:S(2)}) async-start(), calls=%async_computation.2 | async-start | bytes 5242880 | tf_op jit(solution)/shard_map/all_gather | solution.py:36
  12.7 1.1 copy-start
  13.8 133.4 %reduce-scatter.2.cloned.1.call-start = ((), (), s32[]{:S(2)}) async-start(), calls=%async_computation.1 | async-start | bytes 2359296 | tf_op jit(solution)/shard_map/reduce_scatter | solution.py:45
Sparse Core Ops, SparseCore 0:
  13.9 83.4 all-gather.2
  107.6 39.6 reduce-scatter.1
